TPU v7x, 32 devices: a whole 2x2x4 slice. The times are simulated.
32 devices in a mesh: energy: 4 (over y, x), slab: 8 (over z, core).
Axes of the slice: x: 2, y: 2, z: 4, core: 2. Of those that a mesh axis runs over, the one named last changes fastest.
Arguments:
- left_basis: bfloat16 [8, 768, 768], P('slab'), may hold values from -0.21875 to 0.21875
- right_basis: bfloat16 [8, 768, 768], P('slab'), may hold values from -0.21875 to 0.21875
- potential_index: int32 [8], P('slab'), may hold values from 0 to 7
- levels: float32 [8, 768], replicated, may hold values from 0.8 to 1.25
- energy_values: float32 [64], replicated, may hold values from -0.1 to 0.1
- energy_weights: float32 [64], replicated, may hold values from 0.2 to 5
- energy_index: int32 [16], P('energy'), may hold values from 0 to 63
- left_source: bfloat16 [768, 128], replicated, may hold values from -6 to 6
- right_source: bfloat16 [768, 128], replicated, may hold values from -6 to 6
Outputs:
- density: float32 [8, 768], P('slab')
All inputs are finite; a program needn't handle non-finite values.
Results may differ from a plain program's by a relative error of at most 0.0044.
Values may be sent and summed in bfloat16 or wider, within the bound.
A program may use at most 64 MiB of HBM per device.

v0:
```python
import jax
import jax.numpy as jnp
from jax import lax
from jax.sharding import PartitionSpec as P


def passed_along(block, axis, distance):
    devices = range(lax.axis_size(axis))
    route = [(i - distance, i) for i in devices if i - distance in devices]
    return lax.ppermute(block, axis, route)


def local(
    left_basis,
    right_basis,
    potential_index,
    levels,
    energy_values,
    energy_weights,
    energy_index,
    left_source,
    right_source,
):
    slab_count = left_basis.shape[0]
    energy_count = energy_index.shape[0]
    orbitals = left_basis.shape[1]
    modes = left_source.shape[1]
    chain = lax.axis_size("slab")
    position = lax.axis_index("slab")
    total_energies = energy_count * lax.axis_size("energy")
    grid_ids = jnp.arange(energy_values.shape[0], dtype=jnp.int32)
    picked = (energy_index[:, None] == grid_ids[None, :]).astype(jnp.float32)
    energy = jnp.sum(picked * energy_values[None, :], axis=1)
    weight = jnp.sum(picked * energy_weights[None, :], axis=1) / (total_energies * modes)
    profile_ids = jnp.arange(levels.shape[0], dtype=jnp.int32)
    profile = (potential_index[:, None] == profile_ids[None, :]).astype(jnp.float32)
    slab_levels = jnp.sum(profile[:, :, None] * levels[None], axis=1)
    factors_all = 1.0 / (energy[None, :, None] - slab_levels[:, None, :])
    slot_ids = jnp.arange(energy_count, dtype=jnp.int32)

    def select(slot):
        chosen = (slot_ids == slot).astype(jnp.float32)
        return (jnp.sum(chosen[None, :, None] * factors_all, axis=1), jnp.sum(chosen * weight))

    def contribution(state, scale):
        squared = state.astype(jnp.float32) ** 2
        return scale * jnp.sum(squared, axis=1)

    def sweep_down(state, factors, scale):
        mixed = jnp.dot(right_basis[0], state, preferred_element_type=jnp.float32)
        scaled = (factors[0][:, None] * mixed).astype(jnp.bfloat16)
        state = jnp.dot(left_basis[0], scaled, preferred_element_type=jnp.float32).astype(
            jnp.bfloat16
        )
        parts = [contribution(state, scale)]
        return (state, jnp.stack(parts))

    def sweep_up(state, factors, scale):
        parts = []
        for index in reversed(range(slab_count)):
            mixed = jnp.einsum(
                "wv,wm->vm", left_basis[index], state, preferred_element_type=jnp.float32
            )
            scaled = (factors[index][:, None] * mixed).astype(jnp.bfloat16)
            state = jnp.einsum(
                "wv,wm->vm", right_basis[index], scaled, preferred_element_type=jnp.float32
            ).astype(jnp.bfloat16)
            parts.append(contribution(state, scale))
        return (state, jnp.stack(parts[::-1]))

    def forward_work(turn, incoming, state, density):
        start = jnp.where(position == 0, left_source, incoming)
        slot = turn - position
        factors, scale = select(slot)
        active = (slot >= 0) & (slot < energy_count)

        def forward_run(begin):
            fresh, parts = sweep_down(begin, factors, scale)
            return (fresh, density + parts)

        def forward_rest(begin):
            return (state, density)

        return lax.cond(active, forward_run, forward_rest, start)

    def backward_work(turn, incoming, state, density):
        start = jnp.where(position == chain - 1, right_source, incoming)
        slot = turn - (chain - 1 - position)
        factors, scale = select(slot)
        active = (slot >= 0) & (slot < energy_count)

        def backward_run(begin):
            fresh, parts = sweep_up(begin, factors, scale)
            return (fresh, density + parts)

        def backward_rest(begin):
            return (state, density)

        return lax.cond(active, backward_run, backward_rest, start)

    turns = chain + energy_count - 1
    zero_state = jnp.zeros((orbitals, modes), jnp.bfloat16)
    zero_density = jnp.zeros((slab_count, orbitals), jnp.float32)

    def forward_turn(turn, carry):
        state, density = carry
        incoming = passed_along(state, "slab", 1)
        return forward_work(turn, incoming, state, density)

    def backward_turn(turn, carry):
        state, density = carry
        incoming = passed_along(state, "slab", -1)
        return backward_work(turn, incoming, state, density)

    _, forward_density = lax.fori_loop(0, turns, forward_turn, (zero_state, zero_density))
    _, backward_density = lax.fori_loop(0, turns, backward_turn, (zero_state, zero_density))
    return lax.psum(forward_density + backward_density, "energy")


def solution(mesh):
    placed = (
        P("slab", None, None),
        P("slab", None, None),
        P("slab"),
        P(),
        P(),
        P(),
        P("energy"),
        P(),
        P(),
    )
    return jax.shard_map(
        local, mesh=mesh, in_specs=placed, out_specs=P("slab", None), check_vma=False
    )
```

profile of v0, /device:TPU:24, one launch (start us, length us, event | category | flops | bytes accessed | tf_op | source)
XLA Modules:
  0.0 214.1 jit_solution(8526664352582363796)
XLA Ops:
  2.4 93.5 %while.38 = (s32[]{:T(128)}, bf16[768,128]{0,1:T(8,128)(2,1)S(1)}, f32[1,768]{1,0:T(1,128)S(1)}, s32[]{:T(128)}, pred[]{:T(512)}, /*index=5*/bf16[768,128]{1,0:T...) while((s32[]{:T(128)}, bf16[768,128]{0,1:T(8,128)(2,1)S(1)}, ...), condition=%wide.region_16.17_spmd.clone.clone, body=%wide.region_10.16_spmd.clone.clone.sunk | while | flops 302690304 | bytes 4156900 | solution.py:116
  4.6 3.2 %collective-permute-done.1 = bf16[768,128]{1,0:T(8,128)(2,1)S(1)} collective-permute-done((bf16[768,128]{1,0:T(8,128)(2,1)S(1)}, bf16[768,128]{1,0:T(8,128)(2,1)S(1)}, u32[]{:S(2)}, u32[]{:S(2)}) %collective-permute-start.1) | collective-permute-done | bytes 196640 | tf_op jit(solution)/shard_map/while/body/eval_jaxpr/ppermute | solution.py:10
  7.9 3.8 %collective-permute-start.1 = (bf16[768,128]{1,0:T(8,128)(2,1)S(1)}, bf16[768,128]{1,0:T(8,128)(2,1)S(1)}, u32[]{:S(2)}, u32[]{:S(2)}) collective-permute-start(bf16[768,128]{1,0:T(8,128)(2,1)S(1)} %copy.17), channel_id=1, source_target_pairs={{1,0},{2,1},{3,2},{4,3},{5,4},{6,5},{7,6},{9,8},{10,9},{11,10},{12... | collective-permute-start | bytes 589832 | tf_op jit(solution)/shard_map/while/body/eval_jaxpr/ppermute | solution.py:10
  14.9 3.7 %conditional.9 = ((bf16[768,128]{0,1:T(8,128)(2,1)S(1)}, f32[1,768]{1,0:T(1,128)S(1)})) conditional(s32[]{:T(128)} %convert_element_type.149, (bf16[768,128]{0,1:T(8,128)(2,1)S(1)}, f32[1,768]{1,0:T(1,128)S(1)}) %tuple.128, (s32[4]{0:T(128)S(1)}, pred[]{:T(512)}, bf16[768,128]{1,0:T(8,128)(2,1)}, bf16[768,128]{1,0:T(8,128)(2,1)S(1)}, ...), branch_computations={%region_11.11_spmd, %region_12.15_spmd.clone} | conditional | flops 302690304 | bytes 2976905 | solution.py:99
  23.9 3.7 %conditional.9 = ((bf16[768,128]{0,1:T(8,128)(2,1)S(1)}, f32[1,768]{1,0:T(1,128)S(1)})) conditional(s32[]{:T(128)} %convert_element_type.149, (bf16[768,128]{0,1:T(8,128)(2,1)S(1)}, f32[1,768]{1,0:T(1,128)S(1)}) %tuple.128, (s32[4]{0:T(128)S(1)}, pred[]{:T(512)}, bf16[768,128]{1,0:T(8,128)(2,1)}, bf16[768,128]{1,0:T(8,128)(2,1)S(1)}, ...), branch_computations={%region_11.11_spmd, %region_12.15_spmd.clone} | conditional | flops 302690304 | bytes 2976905 | solution.py:99
  27.7 3.8 %collective-permute-start.1 = (bf16[768,128]{1,0:T(8,128)(2,1)S(1)}, bf16[768,128]{1,0:T(8,128)(2,1)S(1)}, u32[]{:S(2)}, u32[]{:S(2)}) collective-permute-start(bf16[768,128]{1,0:T(8,128)(2,1)S(1)} %copy.17), channel_id=1, source_target_pairs={{1,0},{2,1},{3,2},{4,3},{5,4},{6,5},{7,6},{9,8},{10,9},{11,10},{12... | collective-permute-start | bytes 589832 | tf_op jit(solution)/shard_map/while/body/eval_jaxpr/ppermute | solution.py:10
  34.7 3.7 %conditional.9 = ((bf16[768,128]{0,1:T(8,128)(2,1)S(1)}, f32[1,768]{1,0:T(1,128)S(1)})) conditional(s32[]{:T(128)} %convert_element_type.149, (bf16[768,128]{0,1:T(8,128)(2,1)S(1)}, f32[1,768]{1,0:T(1,128)S(1)}) %tuple.128, (s32[4]{0:T(128)S(1)}, pred[]{:T(512)}, bf16[768,128]{1,0:T(8,128)(2,1)}, bf16[768,128]{1,0:T(8,128)(2,1)S(1)}, ...), branch_computations={%region_11.11_spmd, %region_12.15_spmd.clone} | conditional | flops 302690304 | bytes 2976905 | solution.py:99
  38.6 3.8 %collective-permute-start.1 = (bf16[768,128]{1,0:T(8,128)(2,1)S(1)}, bf16[768,128]{1,0:T(8,128)(2,1)S(1)}, u32[]{:S(2)}, u32[]{:S(2)}) collective-permute-start(bf16[768,128]{1,0:T(8,128)(2,1)S(1)} %copy.17), channel_id=1, source_target_pairs={{1,0},{2,1},{3,2},{4,3},{5,4},{6,5},{7,6},{9,8},{10,9},{11,10},{12... | collective-permute-start | bytes 589832 | tf_op jit(solution)/shard_map/while/body/eval_jaxpr/ppermute | solution.py:10
  45.6 3.7 %conditional.9 = ((bf16[768,128]{0,1:T(8,128)(2,1)S(1)}, f32[1,768]{1,0:T(1,128)S(1)})) conditional(s32[]{:T(128)} %convert_element_type.149, (bf16[768,128]{0,1:T(8,128)(2,1)S(1)}, f32[1,768]{1,0:T(1,128)S(1)}) %tuple.128, (s32[4]{0:T(128)S(1)}, pred[]{:T(512)}, bf16[768,128]{1,0:T(8,128)(2,1)}, bf16[768,128]{1,0:T(8,128)(2,1)S(1)}, ...), branch_computations={%region_11.11_spmd, %region_12.15_spmd.clone} | conditional | flops 302690304 | bytes 2976905 | solution.py:99
  49.5 3.8 %collective-permute-start.1 = (bf16[768,128]{1,0:T(8,128)(2,1)S(1)}, bf16[768,128]{1,0:T(8,128)(2,1)S(1)}, u32[]{:S(2)}, u32[]{:S(2)}) collective-permute-start(bf16[768,128]{1,0:T(8,128)(2,1)S(1)} %copy.17), channel_id=1, source_target_pairs={{1,0},{2,1},{3,2},{4,3},{5,4},{6,5},{7,6},{9,8},{10,9},{11,10},{12... | collective-permute-start | bytes 589832 | tf_op jit(solution)/shard_map/while/body/eval_jaxpr/ppermute | solution.py:10
  56.6 7.5 %collective-permute-start.1 = (bf16[768,128]{1,0:T(8,128)(2,1)S(1)}, bf16[768,128]{1,0:T(8,128)(2,1)S(1)}, u32[]{:S(2)}, u32[]{:S(2)}) collective-permute-start(bf16[768,128]{1,0:T(8,128)(2,1)S(1)} %copy.17), channel_id=1, source_target_pairs={{1,0},{2,1},{3,2},{4,3},{5,4},{6,5},{7,6},{9,8},{10,9},{11,10},{12... | collective-permute-start | bytes 589832 | tf_op jit(solution)/shard_map/while/body/eval_jaxpr/ppermute | solution.py:10
  67.5 3.8 %collective-permute-start.1 = (bf16[768,128]{1,0:T(8,128)(2,1)S(1)}, bf16[768,128]{1,0:T(8,128)(2,1)S(1)}, u32[]{:S(2)}, u32[]{:S(2)}) collective-permute-start(bf16[768,128]{1,0:T(8,128)(2,1)S(1)} %copy.17), channel_id=1, source_target_pairs={{1,0},{2,1},{3,2},{4,3},{5,4},{6,5},{7,6},{9,8},{10,9},{11,10},{12... | collective-permute-start | bytes 589832 | tf_op jit(solution)/shard_map/while/body/eval_jaxpr/ppermute | solution.py:10
  74.7 3.8 %collective-permute-start.1 = (bf16[768,128]{1,0:T(8,128)(2,1)S(1)}, bf16[768,128]{1,0:T(8,128)(2,1)S(1)}, u32[]{:S(2)}, u32[]{:S(2)}) collective-permute-start(bf16[768,128]{1,0:T(8,128)(2,1)S(1)} %copy.17), channel_id=1, source_target_pairs={{1,0},{2,1},{3,2},{4,3},{5,4},{6,5},{7,6},{9,8},{10,9},{11,10},{12... | collective-permute-start | bytes 589832 | tf_op jit(solution)/shard_map/while/body/eval_jaxpr/ppermute | solution.py:10
  81.8 3.8 %collective-permute-start.1 = (bf16[768,128]{1,0:T(8,128)(2,1)S(1)}, bf16[768,128]{1,0:T(8,128)(2,1)S(1)}, u32[]{:S(2)}, u32[]{:S(2)}) collective-permute-start(bf16[768,128]{1,0:T(8,128)(2,1)S(1)} %copy.17), channel_id=1, source_target_pairs={{1,0},{2,1},{3,2},{4,3},{5,4},{6,5},{7,6},{9,8},{10,9},{11,10},{12... | collective-permute-start | bytes 589832 | tf_op jit(solution)/shard_map/while/body/eval_jaxpr/ppermute | solution.py:10
  89.0 3.8 %collective-permute-start.1 = (bf16[768,128]{1,0:T(8,128)(2,1)S(1)}, bf16[768,128]{1,0:T(8,128)(2,1)S(1)}, u32[]{:S(2)}, u32[]{:S(2)}) collective-permute-start(bf16[768,128]{1,0:T(8,128)(2,1)S(1)} %copy.17), channel_id=1, source_target_pairs={{1,0},{2,1},{3,2},{4,3},{5,4},{6,5},{7,6},{9,8},{10,9},{11,10},{12... | collective-permute-start | bytes 589832 | tf_op jit(solution)/shard_map/while/body/eval_jaxpr/ppermute | solution.py:10
  96.0 107.6 %while.37 = (s32[]{:T(128)}, bf16[768,128]{0,1:T(8,128)(2,1)S(1)}, f32[1,768]{1,0:T(1,128)S(1)}, s32[]{:T(128)}, pred[]{:T(512)}, /*index=5*/bf16[768,128]{1,0:T...) while((s32[]{:T(128)}, bf16[768,128]{0,1:T(8,128)(2,1)S(1)}, ...), condition=%wide.region_9.10_spmd.clone.clone, body=%wide.region_3.9_spmd.clone.clone.sunk | while | flops 302690304 | bytes 4156900 | solution.py:115
  98.1 5.2 %collective-permute-done = bf16[768,128]{1,0:T(8,128)(2,1)S(1)} collective-permute-done((bf16[768,128]{1,0:T(8,128)(2,1)S(1)}, bf16[768,128]{1,0:T(8,128)(2,1)S(1)}, u32[]{:S(2)}, u32[]{:S(2)}) %collective-permute-start) | collective-permute-done | bytes 196640 | tf_op jit(solution)/shard_map/while/body/eval_jaxpr/ppermute | solution.py:10
  105.4 5.0 %collective-permute-done = bf16[768,128]{1,0:T(8,128)(2,1)S(1)} collective-permute-done((bf16[768,128]{1,0:T(8,128)(2,1)S(1)}, bf16[768,128]{1,0:T(8,128)(2,1)S(1)}, u32[]{:S(2)}, u32[]{:S(2)}) %collective-permute-start) | collective-permute-done | bytes 196640 | tf_op jit(solution)/shard_map/while/body/eval_jaxpr/ppermute | solution.py:10
  112.6 5.0 %collective-permute-done = bf16[768,128]{1,0:T(8,128)(2,1)S(1)} collective-permute-done((bf16[768,128]{1,0:T(8,128)(2,1)S(1)}, bf16[768,128]{1,0:T(8,128)(2,1)S(1)}, u32[]{:S(2)}, u32[]{:S(2)}) %collective-permute-start) | collective-permute-done | bytes 196640 | tf_op jit(solution)/shard_map/while/body/eval_jaxpr/ppermute | solution.py:10
  119.8 5.0 %collective-permute-done = bf16[768,128]{1,0:T(8,128)(2,1)S(1)} collective-permute-done((bf16[768,128]{1,0:T(8,128)(2,1)S(1)}, bf16[768,128]{1,0:T(8,128)(2,1)S(1)}, u32[]{:S(2)}, u32[]{:S(2)}) %collective-permute-start) | collective-permute-done | bytes 196640 | tf_op jit(solution)/shard_map/while/body/eval_jaxpr/ppermute | solution.py:10
  126.9 5.0 %collective-permute-done = bf16[768,128]{1,0:T(8,128)(2,1)S(1)} collective-permute-done((bf16[768,128]{1,0:T(8,128)(2,1)S(1)}, bf16[768,128]{1,0:T(8,128)(2,1)S(1)}, u32[]{:S(2)}, u32[]{:S(2)}) %collective-permute-start) | collective-permute-done | bytes 196640 | tf_op jit(solution)/shard_map/while/body/eval_jaxpr/ppermute | solution.py:10
  134.1 5.0 %collective-permute-done = bf16[768,128]{1,0:T(8,128)(2,1)S(1)} collective-permute-done((bf16[768,128]{1,0:T(8,128)(2,1)S(1)}, bf16[768,128]{1,0:T(8,128)(2,1)S(1)}, u32[]{:S(2)}, u32[]{:S(2)}) %collective-permute-start) | collective-permute-done | bytes 196640 | tf_op jit(solution)/shard_map/while/body/eval_jaxpr/ppermute | solution.py:10
  141.2 18.0 %collective-permute-done = bf16[768,128]{1,0:T(8,128)(2,1)S(1)} collective-permute-done((bf16[768,128]{1,0:T(8,128)(2,1)S(1)}, bf16[768,128]{1,0:T(8,128)(2,1)S(1)}, u32[]{:S(2)}, u32[]{:S(2)}) %collective-permute-start) | collective-permute-done | bytes 196640 | tf_op jit(solution)/shard_map/while/body/eval_jaxpr/ppermute | solution.py:10
  159.3 3.9 %conditional.8 = ((bf16[768,128]{0,1:T(8,128)(2,1)S(1)}, f32[1,768]{1,0:T(1,128)S(1)})) conditional(s32[]{:T(128)} %convert_element_type.148, (bf16[768,128]{0,1:T(8,128)(2,1)S(1)}, f32[1,768]{1,0:T(1,128)S(1)}) %tuple.125, (s32[4]{0:T(128)S(1)}, pred[]{:T(512)}, bf16[768,128]{1,0:T(8,128)(2,1)S(1)}, bf16[768,128]{1,0:T(8,128)(2,1)S(1)}, ...), branch_computations={%region_4.4_spmd, %region_5.8_spmd.clone} | conditional | flops 302690304 | bytes 2976905 | solution.py:84
  165.3 5.1 %collective-permute-done = bf16[768,128]{1,0:T(8,128)(2,1)S(1)} collective-permute-done((bf16[768,128]{1,0:T(8,128)(2,1)S(1)}, bf16[768,128]{1,0:T(8,128)(2,1)S(1)}, u32[]{:S(2)}, u32[]{:S(2)}) %collective-permute-start) | collective-permute-done | bytes 196640 | tf_op jit(solution)/shard_map/while/body/eval_jaxpr/ppermute | solution.py:10
  170.3 3.9 %conditional.8 = ((bf16[768,128]{0,1:T(8,128)(2,1)S(1)}, f32[1,768]{1,0:T(1,128)S(1)})) conditional(s32[]{:T(128)} %convert_element_type.148, (bf16[768,128]{0,1:T(8,128)(2,1)S(1)}, f32[1,768]{1,0:T(1,128)S(1)}) %tuple.125, (s32[4]{0:T(128)S(1)}, pred[]{:T(512)}, bf16[768,128]{1,0:T(8,128)(2,1)S(1)}, bf16[768,128]{1,0:T(8,128)(2,1)S(1)}, ...), branch_computations={%region_4.4_spmd, %region_5.8_spmd.clone} | conditional | flops 302690304 | bytes 2976905 | solution.py:84
  176.4 5.0 %collective-permute-done = bf16[768,128]{1,0:T(8,128)(2,1)S(1)} collective-permute-done((bf16[768,128]{1,0:T(8,128)(2,1)S(1)}, bf16[768,128]{1,0:T(8,128)(2,1)S(1)}, u32[]{:S(2)}, u32[]{:S(2)}) %collective-permute-start) | collective-permute-done | bytes 196640 | tf_op jit(solution)/shard_map/while/body/eval_jaxpr/ppermute | solution.py:10
  181.4 3.9 %conditional.8 = ((bf16[768,128]{0,1:T(8,128)(2,1)S(1)}, f32[1,768]{1,0:T(1,128)S(1)})) conditional(s32[]{:T(128)} %convert_element_type.148, (bf16[768,128]{0,1:T(8,128)(2,1)S(1)}, f32[1,768]{1,0:T(1,128)S(1)}) %tuple.125, (s32[4]{0:T(128)S(1)}, pred[]{:T(512)}, bf16[768,128]{1,0:T(8,128)(2,1)S(1)}, bf16[768,128]{1,0:T(8,128)(2,1)S(1)}, ...), branch_computations={%region_4.4_spmd, %region_5.8_spmd.clone} | conditional | flops 302690304 | bytes 2976905 | solution.py:84
  187.4 5.0 %collective-permute-done = bf16[768,128]{1,0:T(8,128)(2,1)S(1)} collective-permute-done((bf16[768,128]{1,0:T(8,128)(2,1)S(1)}, bf16[768,128]{1,0:T(8,128)(2,1)S(1)}, u32[]{:S(2)}, u32[]{:S(2)}) %collective-permute-start) | collective-permute-done | bytes 196640 | tf_op jit(solution)/shard_map/while/body/eval_jaxpr/ppermute | solution.py:10
  192.5 3.9 %conditional.8 = ((bf16[768,128]{0,1:T(8,128)(2,1)S(1)}, f32[1,768]{1,0:T(1,128)S(1)})) conditional(s32[]{:T(128)} %convert_element_type.148, (bf16[768,128]{0,1:T(8,128)(2,1)S(1)}, f32[1,768]{1,0:T(1,128)S(1)}) %tuple.125, (s32[4]{0:T(128)S(1)}, pred[]{:T(512)}, bf16[768,128]{1,0:T(8,128)(2,1)S(1)}, bf16[768,128]{1,0:T(8,128)(2,1)S(1)}, ...), branch_computations={%region_4.4_spmd, %region_5.8_spmd.clone} | conditional | flops 302690304 | bytes 2976905 | solution.py:84
  198.5 5.0 %collective-permute-done = bf16[768,128]{1,0:T(8,128)(2,1)S(1)} collective-permute-done((bf16[768,128]{1,0:T(8,128)(2,1)S(1)}, bf16[768,128]{1,0:T(8,128)(2,1)S(1)}, u32[]{:S(2)}, u32[]{:S(2)}) %collective-permute-start) | collective-permute-done | bytes 196640 | tf_op jit(solution)/shard_map/while/body/eval_jaxpr/ppermute | solution.py:10
  203.6 10.5 %psum.7 = f32[1,768]{1,0:T(1,128)} all-reduce(f32[1,768]{1,0:T(1,128)S(1)} %add.52), channel_id=1, replica_groups=mesh['energy'=4,'slab'=8] {'energy'}, use_global_device_ids=true, to_apply=%region_17.18 | all-reduce | flops 768 | bytes 6144 | tf_op jit(solution)/shard_map/psum | solution.py:117
  (140 shorter events, 92.0 us)
Async XLA Ops:
  2.4 93.6 %copy-start = (bf16[768,128]{1,0:T(8,128)(2,1)S(1)}, bf16[768,128]{1,0:T(8,128)(2,1)}, u32[]{:S(2)}) copy-start(bf16[768,128]{1,0:T(8,128)(2,1)} %param.24) | copy-start | bytes 589828
  2.6 5.1 %collective-permute-start.1 = (bf16[768,128]{1,0:T(8,128)(2,1)S(1)}, bf16[768,128]{1,0:T(8,128)(2,1)S(1)}, u32[]{:S(2)}, u32[]{:S(2)}) collective-permute-start(bf16[768,128]{1,0:T(8,128)(2,1)S(1)} %copy.17), channel_id=1, source_target_pairs={{1,0},{2,1},{3,2},{4,3},{5,4},{6,5},{7,6},{9,8},{10,9},{11,10},{12... | collective-permute-start | bytes 589832 | tf_op jit(solution)/shard_map/while/body/eval_jaxpr/ppermute | solution.py:10
  7.9 7.0 %collective-permute-start.1 = (bf16[768,128]{1,0:T(8,128)(2,1)S(1)}, bf16[768,128]{1,0:T(8,128)(2,1)S(1)}, u32[]{:S(2)}, u32[]{:S(2)}) collective-permute-start(bf16[768,128]{1,0:T(8,128)(2,1)S(1)} %copy.17), channel_id=1, source_target_pairs={{1,0},{2,1},{3,2},{4,3},{5,4},{6,5},{7,6},{9,8},{10,9},{11,10},{12... | collective-permute-start | bytes 589832 | tf_op jit(solution)/shard_map/while/body/eval_jaxpr/ppermute | solution.py:10
  18.8 5.1 %collective-permute-start.1 = (bf16[768,128]{1,0:T(8,128)(2,1)S(1)}, bf16[768,128]{1,0:T(8,128)(2,1)S(1)}, u32[]{:S(2)}, u32[]{:S(2)}) collective-permute-start(bf16[768,128]{1,0:T(8,128)(2,1)S(1)} %copy.17), channel_id=1, source_target_pairs={{1,0},{2,1},{3,2},{4,3},{5,4},{6,5},{7,6},{9,8},{10,9},{11,10},{12... | collective-permute-start | bytes 589832 | tf_op jit(solution)/shard_map/while/body/eval_jaxpr/ppermute | solution.py:10
  27.7 7.0 %collective-permute-start.1 = (bf16[768,128]{1,0:T(8,128)(2,1)S(1)}, bf16[768,128]{1,0:T(8,128)(2,1)S(1)}, u32[]{:S(2)}, u32[]{:S(2)}) collective-permute-start(bf16[768,128]{1,0:T(8,128)(2,1)S(1)} %copy.17), channel_id=1, source_target_pairs={{1,0},{2,1},{3,2},{4,3},{5,4},{6,5},{7,6},{9,8},{10,9},{11,10},{12... | collective-permute-start | bytes 589832 | tf_op jit(solution)/shard_map/while/body/eval_jaxpr/ppermute | solution.py:10
  38.6 7.0 %collective-permute-start.1 = (bf16[768,128]{1,0:T(8,128)(2,1)S(1)}, bf16[768,128]{1,0:T(8,128)(2,1)S(1)}, u32[]{:S(2)}, u32[]{:S(2)}) collective-permute-start(bf16[768,128]{1,0:T(8,128)(2,1)S(1)} %copy.17), channel_id=1, source_target_pairs={{1,0},{2,1},{3,2},{4,3},{5,4},{6,5},{7,6},{9,8},{10,9},{11,10},{12... | collective-permute-start | bytes 589832 | tf_op jit(solution)/shard_map/while/body/eval_jaxpr/ppermute | solution.py:10
  49.5 7.0 %collective-permute-start.1 = (bf16[768,128]{1,0:T(8,128)(2,1)S(1)}, bf16[768,128]{1,0:T(8,128)(2,1)S(1)}, u32[]{:S(2)}, u32[]{:S(2)}) collective-permute-start(bf16[768,128]{1,0:T(8,128)(2,1)S(1)} %copy.17), channel_id=1, source_target_pairs={{1,0},{2,1},{3,2},{4,3},{5,4},{6,5},{7,6},{9,8},{10,9},{11,10},{12... | collective-permute-start | bytes 589832 | tf_op jit(solution)/shard_map/while/body/eval_jaxpr/ppermute | solution.py:10
  56.6 10.7 %collective-permute-start.1 = (bf16[768,128]{1,0:T(8,128)(2,1)S(1)}, bf16[768,128]{1,0:T(8,128)(2,1)S(1)}, u32[]{:S(2)}, u32[]{:S(2)}) collective-permute-start(bf16[768,128]{1,0:T(8,128)(2,1)S(1)} %copy.17), channel_id=1, source_target_pairs={{1,0},{2,1},{3,2},{4,3},{5,4},{6,5},{7,6},{9,8},{10,9},{11,10},{12... | collective-permute-start | bytes 589832 | tf_op jit(solution)/shard_map/while/body/eval_jaxpr/ppermute | solution.py:10
  67.5 7.0 %collective-permute-start.1 = (bf16[768,128]{1,0:T(8,128)(2,1)S(1)}, bf16[768,128]{1,0:T(8,128)(2,1)S(1)}, u32[]{:S(2)}, u32[]{:S(2)}) collective-permute-start(bf16[768,128]{1,0:T(8,128)(2,1)S(1)} %copy.17), channel_id=1, source_target_pairs={{1,0},{2,1},{3,2},{4,3},{5,4},{6,5},{7,6},{9,8},{10,9},{11,10},{12... | collective-permute-start | bytes 589832 | tf_op jit(solution)/shard_map/while/body/eval_jaxpr/ppermute | solution.py:10
  74.7 7.0 %collective-permute-start.1 = (bf16[768,128]{1,0:T(8,128)(2,1)S(1)}, bf16[768,128]{1,0:T(8,128)(2,1)S(1)}, u32[]{:S(2)}, u32[]{:S(2)}) collective-permute-start(bf16[768,128]{1,0:T(8,128)(2,1)S(1)} %copy.17), channel_id=1, source_target_pairs={{1,0},{2,1},{3,2},{4,3},{5,4},{6,5},{7,6},{9,8},{10,9},{11,10},{12... | collective-permute-start | bytes 589832 | tf_op jit(solution)/shard_map/while/body/eval_jaxpr/ppermute | solution.py:10
  81.8 7.0 %collective-permute-start.1 = (bf16[768,128]{1,0:T(8,128)(2,1)S(1)}, bf16[768,128]{1,0:T(8,128)(2,1)S(1)}, u32[]{:S(2)}, u32[]{:S(2)}) collective-permute-start(bf16[768,128]{1,0:T(8,128)(2,1)S(1)} %copy.17), channel_id=1, source_target_pairs={{1,0},{2,1},{3,2},{4,3},{5,4},{6,5},{7,6},{9,8},{10,9},{11,10},{12... | collective-permute-start | bytes 589832 | tf_op jit(solution)/shard_map/while/body/eval_jaxpr/ppermute | solution.py:10
  89.0 7.0 %collective-permute-start.1 = (bf16[768,128]{1,0:T(8,128)(2,1)S(1)}, bf16[768,128]{1,0:T(8,128)(2,1)S(1)}, u32[]{:S(2)}, u32[]{:S(2)}) collective-permute-start(bf16[768,128]{1,0:T(8,128)(2,1)S(1)} %copy.17), channel_id=1, source_target_pairs={{1,0},{2,1},{3,2},{4,3},{5,4},{6,5},{7,6},{9,8},{10,9},{11,10},{12... | collective-permute-start | bytes 589832 | tf_op jit(solution)/shard_map/while/body/eval_jaxpr/ppermute | solution.py:10
  96.2 7.2 %collective-permute-start = (bf16[768,128]{1,0:T(8,128)(2,1)S(1)}, bf16[768,128]{1,0:T(8,128)(2,1)S(1)}, u32[]{:S(2)}, u32[]{:S(2)}) collective-permute-start(bf16[768,128]{1,0:T(8,128)(2,1)S(1)} %copy.16), channel_id=1, source_target_pairs={{0,1},{1,2},{2,3},{3,4},{4,5},{5,6},{6,7},{8,9},{9,10},{10,11},{11... | collective-permute-start | bytes 589832 | tf_op jit(solution)/shard_map/while/body/eval_jaxpr/ppermute | solution.py:10
  103.5 7.0 %collective-permute-start = (bf16[768,128]{1,0:T(8,128)(2,1)S(1)}, bf16[768,128]{1,0:T(8,128)(2,1)S(1)}, u32[]{:S(2)}, u32[]{:S(2)}) collective-permute-start(bf16[768,128]{1,0:T(8,128)(2,1)S(1)} %copy.16), channel_id=1, source_target_pairs={{0,1},{1,2},{2,3},{3,4},{4,5},{5,6},{6,7},{8,9},{9,10},{10,11},{11... | collective-permute-start | bytes 589832 | tf_op jit(solution)/shard_map/while/body/eval_jaxpr/ppermute | solution.py:10
  110.7 7.0 %collective-permute-start = (bf16[768,128]{1,0:T(8,128)(2,1)S(1)}, bf16[768,128]{1,0:T(8,128)(2,1)S(1)}, u32[]{:S(2)}, u32[]{:S(2)}) collective-permute-start(bf16[768,128]{1,0:T(8,128)(2,1)S(1)} %copy.16), channel_id=1, source_target_pairs={{0,1},{1,2},{2,3},{3,4},{4,5},{5,6},{6,7},{8,9},{9,10},{10,11},{11... | collective-permute-start | bytes 589832 | tf_op jit(solution)/shard_map/while/body/eval_jaxpr/ppermute | solution.py:10
  117.8 7.0 %collective-permute-start = (bf16[768,128]{1,0:T(8,128)(2,1)S(1)}, bf16[768,128]{1,0:T(8,128)(2,1)S(1)}, u32[]{:S(2)}, u32[]{:S(2)}) collective-permute-start(bf16[768,128]{1,0:T(8,128)(2,1)S(1)} %copy.16), channel_id=1, source_target_pairs={{0,1},{1,2},{2,3},{3,4},{4,5},{5,6},{6,7},{8,9},{9,10},{10,11},{11... | collective-permute-start | bytes 589832 | tf_op jit(solution)/shard_map/while/body/eval_jaxpr/ppermute | solution.py:10
  125.0 7.0 %collective-permute-start = (bf16[768,128]{1,0:T(8,128)(2,1)S(1)}, bf16[768,128]{1,0:T(8,128)(2,1)S(1)}, u32[]{:S(2)}, u32[]{:S(2)}) collective-permute-start(bf16[768,128]{1,0:T(8,128)(2,1)S(1)} %copy.16), channel_id=1, source_target_pairs={{0,1},{1,2},{2,3},{3,4},{4,5},{5,6},{6,7},{8,9},{9,10},{10,11},{11... | collective-permute-start | bytes 589832 | tf_op jit(solution)/shard_map/while/body/eval_jaxpr/ppermute | solution.py:10
  132.1 7.0 %collective-permute-start = (bf16[768,128]{1,0:T(8,128)(2,1)S(1)}, bf16[768,128]{1,0:T(8,128)(2,1)S(1)}, u32[]{:S(2)}, u32[]{:S(2)}) collective-permute-start(bf16[768,128]{1,0:T(8,128)(2,1)S(1)} %copy.16), channel_id=1, source_target_pairs={{0,1},{1,2},{2,3},{3,4},{4,5},{5,6},{6,7},{8,9},{9,10},{10,11},{11... | collective-permute-start | bytes 589832 | tf_op jit(solution)/shard_map/while/body/eval_jaxpr/ppermute | solution.py:10
  139.3 20.0 %collective-permute-start = (bf16[768,128]{1,0:T(8,128)(2,1)S(1)}, bf16[768,128]{1,0:T(8,128)(2,1)S(1)}, u32[]{:S(2)}, u32[]{:S(2)}) collective-permute-start(bf16[768,128]{1,0:T(8,128)(2,1)S(1)} %copy.16), channel_id=1, source_target_pairs={{0,1},{1,2},{2,3},{3,4},{4,5},{5,6},{6,7},{8,9},{9,10},{10,11},{11... | collective-permute-start | bytes 589832 | tf_op jit(solution)/shard_map/while/body/eval_jaxpr/ppermute | solution.py:10
  163.3 7.0 %collective-permute-start = (bf16[768,128]{1,0:T(8,128)(2,1)S(1)}, bf16[768,128]{1,0:T(8,128)(2,1)S(1)}, u32[]{:S(2)}, u32[]{:S(2)}) collective-permute-start(bf16[768,128]{1,0:T(8,128)(2,1)S(1)} %copy.16), channel_id=1, source_target_pairs={{0,1},{1,2},{2,3},{3,4},{4,5},{5,6},{6,7},{8,9},{9,10},{10,11},{11... | collective-permute-start | bytes 589832 | tf_op jit(solution)/shard_map/while/body/eval_jaxpr/ppermute | solution.py:10
  174.4 7.0 %collective-permute-start = (bf16[768,128]{1,0:T(8,128)(2,1)S(1)}, bf16[768,128]{1,0:T(8,128)(2,1)S(1)}, u32[]{:S(2)}, u32[]{:S(2)}) collective-permute-start(bf16[768,128]{1,0:T(8,128)(2,1)S(1)} %copy.16), channel_id=1, source_target_pairs={{0,1},{1,2},{2,3},{3,4},{4,5},{5,6},{6,7},{8,9},{9,10},{10,11},{11... | collective-permute-start | bytes 589832 | tf_op jit(solution)/shard_map/while/body/eval_jaxpr/ppermute | solution.py:10
  185.5 7.0 %collective-permute-start = (bf16[768,128]{1,0:T(8,128)(2,1)S(1)}, bf16[768,128]{1,0:T(8,128)(2,1)S(1)}, u32[]{:S(2)}, u32[]{:S(2)}) collective-permute-start(bf16[768,128]{1,0:T(8,128)(2,1)S(1)} %copy.16), channel_id=1, source_target_pairs={{0,1},{1,2},{2,3},{3,4},{4,5},{5,6},{6,7},{8,9},{9,10},{10,11},{11... | collective-permute-start | bytes 589832 | tf_op jit(solution)/shard_map/while/body/eval_jaxpr/ppermute | solution.py:10
  196.6 7.0 %collective-permute-start = (bf16[768,128]{1,0:T(8,128)(2,1)S(1)}, bf16[768,128]{1,0:T(8,128)(2,1)S(1)}, u32[]{:S(2)}, u32[]{:S(2)}) collective-permute-start(bf16[768,128]{1,0:T(8,128)(2,1)S(1)} %copy.16), channel_id=1, source_target_pairs={{0,1},{1,2},{2,3},{3,4},{4,5},{5,6},{6,7},{8,9},{9,10},{10,11},{11... | collective-permute-start | bytes 589832 | tf_op jit(solution)/shard_map/while/body/eval_jaxpr/ppermute | solution.py:10
where the time goes:
time: 215 us; the launch traced here: 214 us
  waiting for transfers between devices  103 us (48%)
  starting transfers between devices  63 us (29%)
  matrix products  19.5 us (9%)
  other arithmetic  12.4 us (6%)
  blocking collectives  10.5 us (5%)
  local copies, waits for them, and re-layouts  3.61 us (2%)
    ppermute x22, waiting for transfers between devices, passed_along(): return lax.ppermute(block, axis, route)  103 us
    ppermute x22, starting transfers between devices, passed_along(): return lax.ppermute(block, axis, route)  63 us
    psum x1, blocking collectives, local(): return lax.psum(forward_density + backward_density, 'energy')  10.5 us
    dot_general x4, matrix products, sweep_down(): jnp.dot(left_basis[0], scaled, preferred_element_type=jnp.float32)  10.1 us
    dot_general x4, matrix products, sweep_up(): jnp.einsum('wv,wm->vm', right_basis[index], scaled, preferred_element_typ...  9.33 us
    reduce_sum x8, other arithmetic, select(): jnp.sum(chosen * weight)  4.96 us
    mul x8, other arithmetic, contribution(): return scale * jnp.sum(squared, axis=1)  4.91 us
  transfers between devices with their start and end apart: 22, of which 22 were waited for; matrix products, arithmetic and copies ran while one was open for 0% of the time, Pallas kernels for 0%

commit v1 on v0

--- a/solution.py
+++ b/solution.py
@@ -114,7 +114,7 @@
 
     _, forward_density = lax.fori_loop(0, turns, forward_turn, (zero_state, zero_density))
     _, backward_density = lax.fori_loop(0, turns, backward_turn, (zero_state, zero_density))
-    return lax.psum(forward_density + backward_density, "energy")
+    return jnp.sum(lax.all_gather(forward_density + backward_density, "energy"), axis=0)
 
 
 def solution(mesh):

time: 215 us -> 213 us (level)
  blocking collectives: 10.5 us -> 8.16 us
    psum x1 -> x0, blocking collectives: 10.5 us -> none  [local(): return lax.psum(forward_density + backward_density, 'energy')]
    all_gather x0 -> x1, blocking collectives: none -> 8.16 us  [local(): lax.all_gather(forward_density + backward_density, 'energy')]
where the time goes in v1:
time: 213 us; the launch traced here: 212 us
  waiting for transfers between devices  103 us (48%)
  starting transfers between devices  63 us (30%)
  matrix products  19.5 us (9%)
  other arithmetic  12.5 us (6%)
  blocking collectives  8.16 us (4%)
  local copies, waits for them, and re-layouts  4.19 us (2%)
    ppermute x22, waiting for transfers between devices, passed_along(): return lax.ppermute(block, axis, route)  103 us
    ppermute x22, starting transfers between devices, passed_along(): return lax.ppermute(block, axis, route)  63 us
    dot_general x4, matrix products, sweep_down(): jnp.dot(left_basis[0], scaled, preferred_element_type=jnp.float32)  10.1 us
    dot_general x4, matrix products, sweep_up(): jnp.einsum('wv,wm->vm', right_basis[index], scaled, preferred_element_typ...  9.33 us
    all_gather x1, blocking collectives, local(): lax.all_gather(forward_density + backward_density, 'energy')  8.16 us
    reduce_sum x8, other arithmetic, select(): jnp.sum(chosen * weight)  4.96 us
    mul x8, other arithmetic, contribution(): return scale * jnp.sum(squared, axis=1)  4.91 us
  transfers between devices with their start and end apart: 22, of which 22 were waited for; matrix products, arithmetic and copies ran while one was open for 0% of the time, Pallas kernels for 0%

profile of v1, /device:TPU:24, one launch (start us, length us, event | category | flops | bytes accessed | tf_op | source)
XLA Modules:
  0.0 212.3 jit_solution(15903932243232067528)
XLA Ops:
  2.4 93.5 %while.38 = (s32[]{:T(128)}, bf16[768,128]{0,1:T(8,128)(2,1)S(1)}, f32[1,768]{1,0:T(1,128)S(1)}, s32[]{:T(128)}, pred[]{:T(512)}, /*index=5*/bf16[768,128]{1,0:T...) while((s32[]{:T(128)}, bf16[768,128]{0,1:T(8,128)(2,1)S(1)}, ...), condition=%wide.region_16.17_spmd.clone.clone, body=%wide.region_10.16_spmd.clone.clone.sunk | while | flops 302690304 | bytes 4156900 | solution.py:116
  4.6 3.2 %collective-permute-done.1 = bf16[768,128]{1,0:T(8,128)(2,1)S(1)} collective-permute-done((bf16[768,128]{1,0:T(8,128)(2,1)S(1)}, bf16[768,128]{1,0:T(8,128)(2,1)S(1)}, u32[]{:S(2)}, u32[]{:S(2)}) %collective-permute-start.1) | collective-permute-done | bytes 196640 | tf_op jit(solution)/shard_map/while/body/eval_jaxpr/ppermute | solution.py:10
  7.9 3.8 %collective-permute-start.1 = (bf16[768,128]{1,0:T(8,128)(2,1)S(1)}, bf16[768,128]{1,0:T(8,128)(2,1)S(1)}, u32[]{:S(2)}, u32[]{:S(2)}) collective-permute-start(bf16[768,128]{1,0:T(8,128)(2,1)S(1)} %copy.19), channel_id=1, source_target_pairs={{1,0},{2,1},{3,2},{4,3},{5,4},{6,5},{7,6},{9,8},{10,9},{11,10},{12... | collective-permute-start | bytes 589832 | tf_op jit(solution)/shard_map/while/body/eval_jaxpr/ppermute | solution.py:10
  14.9 3.7 %conditional.9 = ((bf16[768,128]{0,1:T(8,128)(2,1)S(1)}, f32[1,768]{1,0:T(1,128)S(1)})) conditional(s32[]{:T(128)} %convert_element_type.149, (bf16[768,128]{0,1:T(8,128)(2,1)S(1)}, f32[1,768]{1,0:T(1,128)S(1)}) %tuple.128, (s32[4]{0:T(128)S(1)}, pred[]{:T(512)}, bf16[768,128]{1,0:T(8,128)(2,1)}, bf16[768,128]{1,0:T(8,128)(2,1)S(1)}, ...), branch_computations={%region_11.11_spmd, %region_12.15_spmd.clone} | conditional | flops 302690304 | bytes 2976905 | solution.py:99
  23.9 3.7 %conditional.9 = ((bf16[768,128]{0,1:T(8,128)(2,1)S(1)}, f32[1,768]{1,0:T(1,128)S(1)})) conditional(s32[]{:T(128)} %convert_element_type.149, (bf16[768,128]{0,1:T(8,128)(2,1)S(1)}, f32[1,768]{1,0:T(1,128)S(1)}) %tuple.128, (s32[4]{0:T(128)S(1)}, pred[]{:T(512)}, bf16[768,128]{1,0:T(8,128)(2,1)}, bf16[768,128]{1,0:T(8,128)(2,1)S(1)}, ...), branch_computations={%region_11.11_spmd, %region_12.15_spmd.clone} | conditional | flops 302690304 | bytes 2976905 | solution.py:99
  27.7 3.8 %collective-permute-start.1 = (bf16[768,128]{1,0:T(8,128)(2,1)S(1)}, bf16[768,128]{1,0:T(8,128)(2,1)S(1)}, u32[]{:S(2)}, u32[]{:S(2)}) collective-permute-start(bf16[768,128]{1,0:T(8,128)(2,1)S(1)} %copy.19), channel_id=1, source_target_pairs={{1,0},{2,1},{3,2},{4,3},{5,4},{6,5},{7,6},{9,8},{10,9},{11,10},{12... | collective-permute-start | bytes 589832 | tf_op jit(solution)/shard_map/while/body/eval_jaxpr/ppermute | solution.py:10
  34.7 3.7 %conditional.9 = ((bf16[768,128]{0,1:T(8,128)(2,1)S(1)}, f32[1,768]{1,0:T(1,128)S(1)})) conditional(s32[]{:T(128)} %convert_element_type.149, (bf16[768,128]{0,1:T(8,128)(2,1)S(1)}, f32[1,768]{1,0:T(1,128)S(1)}) %tuple.128, (s32[4]{0:T(128)S(1)}, pred[]{:T(512)}, bf16[768,128]{1,0:T(8,128)(2,1)}, bf16[768,128]{1,0:T(8,128)(2,1)S(1)}, ...), branch_computations={%region_11.11_spmd, %region_12.15_spmd.clone} | conditional | flops 302690304 | bytes 2976905 | solution.py:99
  38.6 3.8 %collective-permute-start.1 = (bf16[768,128]{1,0:T(8,128)(2,1)S(1)}, bf16[768,128]{1,0:T(8,128)(2,1)S(1)}, u32[]{:S(2)}, u32[]{:S(2)}) collective-permute-start(bf16[768,128]{1,0:T(8,128)(2,1)S(1)} %copy.19), channel_id=1, source_target_pairs={{1,0},{2,1},{3,2},{4,3},{5,4},{6,5},{7,6},{9,8},{10,9},{11,10},{12... | collective-permute-start | bytes 589832 | tf_op jit(solution)/shard_map/while/body/eval_jaxpr/ppermute | solution.py:10
  45.6 3.7 %conditional.9 = ((bf16[768,128]{0,1:T(8,128)(2,1)S(1)}, f32[1,768]{1,0:T(1,128)S(1)})) conditional(s32[]{:T(128)} %convert_element_type.149, (bf16[768,128]{0,1:T(8,128)(2,1)S(1)}, f32[1,768]{1,0:T(1,128)S(1)}) %tuple.128, (s32[4]{0:T(128)S(1)}, pred[]{:T(512)}, bf16[768,128]{1,0:T(8,128)(2,1)}, bf16[768,128]{1,0:T(8,128)(2,1)S(1)}, ...), branch_computations={%region_11.11_spmd, %region_12.15_spmd.clone} | conditional | flops 302690304 | bytes 2976905 | solution.py:99
  49.5 3.8 %collective-permute-start.1 = (bf16[768,128]{1,0:T(8,128)(2,1)S(1)}, bf16[768,128]{1,0:T(8,128)(2,1)S(1)}, u32[]{:S(2)}, u32[]{:S(2)}) collective-permute-start(bf16[768,128]{1,0:T(8,128)(2,1)S(1)} %copy.19), channel_id=1, source_target_pairs={{1,0},{2,1},{3,2},{4,3},{5,4},{6,5},{7,6},{9,8},{10,9},{11,10},{12... | collective-permute-start | bytes 589832 | tf_op jit(solution)/shard_map/while/body/eval_jaxpr/ppermute | solution.py:10
  56.6 7.5 %collective-permute-start.1 = (bf16[768,128]{1,0:T(8,128)(2,1)S(1)}, bf16[768,128]{1,0:T(8,128)(2,1)S(1)}, u32[]{:S(2)}, u32[]{:S(2)}) collective-permute-start(bf16[768,128]{1,0:T(8,128)(2,1)S(1)} %copy.19), channel_id=1, source_target_pairs={{1,0},{2,1},{3,2},{4,3},{5,4},{6,5},{7,6},{9,8},{10,9},{11,10},{12... | collective-permute-start | bytes 589832 | tf_op jit(solution)/shard_map/while/body/eval_jaxpr/ppermute | solution.py:10
  67.5 3.8 %collective-permute-start.1 = (bf16[768,128]{1,0:T(8,128)(2,1)S(1)}, bf16[768,128]{1,0:T(8,128)(2,1)S(1)}, u32[]{:S(2)}, u32[]{:S(2)}) collective-permute-start(bf16[768,128]{1,0:T(8,128)(2,1)S(1)} %copy.19), channel_id=1, source_target_pairs={{1,0},{2,1},{3,2},{4,3},{5,4},{6,5},{7,6},{9,8},{10,9},{11,10},{12... | collective-permute-start | bytes 589832 | tf_op jit(solution)/shard_map/while/body/eval_jaxpr/ppermute | solution.py:10
  74.7 3.8 %collective-permute-start.1 = (bf16[768,128]{1,0:T(8,128)(2,1)S(1)}, bf16[768,128]{1,0:T(8,128)(2,1)S(1)}, u32[]{:S(2)}, u32[]{:S(2)}) collective-permute-start(bf16[768,128]{1,0:T(8,128)(2,1)S(1)} %copy.19), channel_id=1, source_target_pairs={{1,0},{2,1},{3,2},{4,3},{5,4},{6,5},{7,6},{9,8},{10,9},{11,10},{12... | collective-permute-start | bytes 589832 | tf_op jit(solution)/shard_map/while/body/eval_jaxpr/ppermute | solution.py:10
  81.8 3.8 %collective-permute-start.1 = (bf16[768,128]{1,0:T(8,128)(2,1)S(1)}, bf16[768,128]{1,0:T(8,128)(2,1)S(1)}, u32[]{:S(2)}, u32[]{:S(2)}) collective-permute-start(bf16[768,128]{1,0:T(8,128)(2,1)S(1)} %copy.19), channel_id=1, source_target_pairs={{1,0},{2,1},{3,2},{4,3},{5,4},{6,5},{7,6},{9,8},{10,9},{11,10},{12... | collective-permute-start | bytes 589832 | tf_op jit(solution)/shard_map/while/body/eval_jaxpr/ppermute | solution.py:10
  89.0 3.8 %collective-permute-start.1 = (bf16[768,128]{1,0:T(8,128)(2,1)S(1)}, bf16[768,128]{1,0:T(8,128)(2,1)S(1)}, u32[]{:S(2)}, u32[]{:S(2)}) collective-permute-start(bf16[768,128]{1,0:T(8,128)(2,1)S(1)} %copy.19), channel_id=1, source_target_pairs={{1,0},{2,1},{3,2},{4,3},{5,4},{6,5},{7,6},{9,8},{10,9},{11,10},{12... | collective-permute-start | bytes 589832 | tf_op jit(solution)/shard_map/while/body/eval_jaxpr/ppermute | solution.py:10
  96.0 107.6 %while.37 = (s32[]{:T(128)}, bf16[768,128]{0,1:T(8,128)(2,1)S(1)}, f32[1,768]{1,0:T(1,128)S(1)}, s32[]{:T(128)}, pred[]{:T(512)}, /*index=5*/bf16[768,128]{1,0:T...) while((s32[]{:T(128)}, bf16[768,128]{0,1:T(8,128)(2,1)S(1)}, ...), condition=%wide.region_9.10_spmd.clone.clone, body=%wide.region_3.9_spmd.clone.clone.sunk | while | flops 302690304 | bytes 4156900 | solution.py:115
  98.1 5.2 %collective-permute-done = bf16[768,128]{1,0:T(8,128)(2,1)S(1)} collective-permute-done((bf16[768,128]{1,0:T(8,128)(2,1)S(1)}, bf16[768,128]{1,0:T(8,128)(2,1)S(1)}, u32[]{:S(2)}, u32[]{:S(2)}) %collective-permute-start) | collective-permute-done | bytes 196640 | tf_op jit(solution)/shard_map/while/body/eval_jaxpr/ppermute | solution.py:10
  105.4 5.0 %collective-permute-done = bf16[768,128]{1,0:T(8,128)(2,1)S(1)} collective-permute-done((bf16[768,128]{1,0:T(8,128)(2,1)S(1)}, bf16[768,128]{1,0:T(8,128)(2,1)S(1)}, u32[]{:S(2)}, u32[]{:S(2)}) %collective-permute-start) | collective-permute-done | bytes 196640 | tf_op jit(solution)/shard_map/while/body/eval_jaxpr/ppermute | solution.py:10
  112.6 5.0 %collective-permute-done = bf16[768,128]{1,0:T(8,128)(2,1)S(1)} collective-permute-done((bf16[768,128]{1,0:T(8,128)(2,1)S(1)}, bf16[768,128]{1,0:T(8,128)(2,1)S(1)}, u32[]{:S(2)}, u32[]{:S(2)}) %collective-permute-start) | collective-permute-done | bytes 196640 | tf_op jit(solution)/shard_map/while/body/eval_jaxpr/ppermute | solution.py:10
  119.8 5.0 %collective-permute-done = bf16[768,128]{1,0:T(8,128)(2,1)S(1)} collective-permute-done((bf16[768,128]{1,0:T(8,128)(2,1)S(1)}, bf16[768,128]{1,0:T(8,128)(2,1)S(1)}, u32[]{:S(2)}, u32[]{:S(2)}) %collective-permute-start) | collective-permute-done | bytes 196640 | tf_op jit(solution)/shard_map/while/body/eval_jaxpr/ppermute | solution.py:10
  126.9 5.0 %collective-permute-done = bf16[768,128]{1,0:T(8,128)(2,1)S(1)} collective-permute-done((bf16[768,128]{1,0:T(8,128)(2,1)S(1)}, bf16[768,128]{1,0:T(8,128)(2,1)S(1)}, u32[]{:S(2)}, u32[]{:S(2)}) %collective-permute-start) | collective-permute-done | bytes 196640 | tf_op jit(solution)/shard_map/while/body/eval_jaxpr/ppermute | solution.py:10
  134.1 5.0 %collective-permute-done = bf16[768,128]{1,0:T(8,128)(2,1)S(1)} collective-permute-done((bf16[768,128]{1,0:T(8,128)(2,1)S(1)}, bf16[768,128]{1,0:T(8,128)(2,1)S(1)}, u32[]{:S(2)}, u32[]{:S(2)}) %collective-permute-start) | collective-permute-done | bytes 196640 | tf_op jit(solution)/shard_map/while/body/eval_jaxpr/ppermute | solution.py:10
  141.2 18.0 %collective-permute-done = bf16[768,128]{1,0:T(8,128)(2,1)S(1)} collective-permute-done((bf16[768,128]{1,0:T(8,128)(2,1)S(1)}, bf16[768,128]{1,0:T(8,128)(2,1)S(1)}, u32[]{:S(2)}, u32[]{:S(2)}) %collective-permute-start) | collective-permute-done | bytes 196640 | tf_op jit(solution)/shard_map/while/body/eval_jaxpr/ppermute | solution.py:10
  159.3 3.9 %conditional.8 = ((bf16[768,128]{0,1:T(8,128)(2,1)S(1)}, f32[1,768]{1,0:T(1,128)S(1)})) conditional(s32[]{:T(128)} %convert_element_type.148, (bf16[768,128]{0,1:T(8,128)(2,1)S(1)}, f32[1,768]{1,0:T(1,128)S(1)}) %tuple.125, (s32[4]{0:T(128)S(1)}, pred[]{:T(512)}, bf16[768,128]{1,0:T(8,128)(2,1)S(1)}, bf16[768,128]{1,0:T(8,128)(2,1)S(1)}, ...), branch_computations={%region_4.4_spmd, %region_5.8_spmd.clone} | conditional | flops 302690304 | bytes 2976905 | solution.py:84
  165.3 5.1 %collective-permute-done = bf16[768,128]{1,0:T(8,128)(2,1)S(1)} collective-permute-done((bf16[768,128]{1,0:T(8,128)(2,1)S(1)}, bf16[768,128]{1,0:T(8,128)(2,1)S(1)}, u32[]{:S(2)}, u32[]{:S(2)}) %collective-permute-start) | collective-permute-done | bytes 196640 | tf_op jit(solution)/shard_map/while/body/eval_jaxpr/ppermute | solution.py:10
  170.3 3.9 %conditional.8 = ((bf16[768,128]{0,1:T(8,128)(2,1)S(1)}, f32[1,768]{1,0:T(1,128)S(1)})) conditional(s32[]{:T(128)} %convert_element_type.148, (bf16[768,128]{0,1:T(8,128)(2,1)S(1)}, f32[1,768]{1,0:T(1,128)S(1)}) %tuple.125, (s32[4]{0:T(128)S(1)}, pred[]{:T(512)}, bf16[768,128]{1,0:T(8,128)(2,1)S(1)}, bf16[768,128]{1,0:T(8,128)(2,1)S(1)}, ...), branch_computations={%region_4.4_spmd, %region_5.8_spmd.clone} | conditional | flops 302690304 | bytes 2976905 | solution.py:84
  176.4 5.0 %collective-permute-done = bf16[768,128]{1,0:T(8,128)(2,1)S(1)} collective-permute-done((bf16[768,128]{1,0:T(8,128)(2,1)S(1)}, bf16[768,128]{1,0:T(8,128)(2,1)S(1)}, u32[]{:S(2)}, u32[]{:S(2)}) %collective-permute-start) | collective-permute-done | bytes 196640 | tf_op jit(solution)/shard_map/while/body/eval_jaxpr/ppermute | solution.py:10
  181.4 3.9 %conditional.8 = ((bf16[768,128]{0,1:T(8,128)(2,1)S(1)}, f32[1,768]{1,0:T(1,128)S(1)})) conditional(s32[]{:T(128)} %convert_element_type.148, (bf16[768,128]{0,1:T(8,128)(2,1)S(1)}, f32[1,768]{1,0:T(1,128)S(1)}) %tuple.125, (s32[4]{0:T(128)S(1)}, pred[]{:T(512)}, bf16[768,128]{1,0:T(8,128)(2,1)S(1)}, bf16[768,128]{1,0:T(8,128)(2,1)S(1)}, ...), branch_computations={%region_4.4_spmd, %region_5.8_spmd.clone} | conditional | flops 302690304 | bytes 2976905 | solution.py:84
  187.4 5.0 %collective-permute-done = bf16[768,128]{1,0:T(8,128)(2,1)S(1)} collective-permute-done((bf16[768,128]{1,0:T(8,128)(2,1)S(1)}, bf16[768,128]{1,0:T(8,128)(2,1)S(1)}, u32[]{:S(2)}, u32[]{:S(2)}) %collective-permute-start) | collective-permute-done | bytes 196640 | tf_op jit(solution)/shard_map/while/body/eval_jaxpr/ppermute | solution.py:10
  192.5 3.9 %conditional.8 = ((bf16[768,128]{0,1:T(8,128)(2,1)S(1)}, f32[1,768]{1,0:T(1,128)S(1)})) conditional(s32[]{:T(128)} %convert_element_type.148, (bf16[768,128]{0,1:T(8,128)(2,1)S(1)}, f32[1,768]{1,0:T(1,128)S(1)}) %tuple.125, (s32[4]{0:T(128)S(1)}, pred[]{:T(512)}, bf16[768,128]{1,0:T(8,128)(2,1)S(1)}, bf16[768,128]{1,0:T(8,128)(2,1)S(1)}, ...), branch_computations={%region_4.4_spmd, %region_5.8_spmd.clone} | conditional | flops 302690304 | bytes 2976905 | solution.py:84
  198.5 5.0 %collective-permute-done = bf16[768,128]{1,0:T(8,128)(2,1)S(1)} collective-permute-done((bf16[768,128]{1,0:T(8,128)(2,1)S(1)}, bf16[768,128]{1,0:T(8,128)(2,1)S(1)}, u32[]{:S(2)}, u32[]{:S(2)}) %collective-permute-start) | collective-permute-done | bytes 196640 | tf_op jit(solution)/shard_map/while/body/eval_jaxpr/ppermute | solution.py:10
  203.6 8.2 %all-gather.1 = f32[4,1,768]{2,1,0:T(1,128)S(1)} all-gather(f32[1,1,768]{2,1,0:T(1,128)S(1)} %add_bitcast_fusion), channel_id=2, replica_groups=mesh['energy'=4,'slab'=8] {'energy'}, dimensions={0}, use_global_device_ids=true | all-gather | bytes 15360 | tf_op jit(solution)/shard_map/all_gather | solution.py:117
  (142 shorter events, 92.6 us)
Async XLA Ops:
  2.4 93.6 %copy-start = (bf16[768,128]{1,0:T(8,128)(2,1)S(1)}, bf16[768,128]{1,0:T(8,128)(2,1)}, u32[]{:S(2)}) copy-start(bf16[768,128]{1,0:T(8,128)(2,1)} %param.24) | copy-start | bytes 589828
  2.6 5.1 %collective-permute-start.1 = (bf16[768,128]{1,0:T(8,128)(2,1)S(1)}, bf16[768,128]{1,0:T(8,128)(2,1)S(1)}, u32[]{:S(2)}, u32[]{:S(2)}) collective-permute-start(bf16[768,128]{1,0:T(8,128)(2,1)S(1)} %copy.19), channel_id=1, source_target_pairs={{1,0},{2,1},{3,2},{4,3},{5,4},{6,5},{7,6},{9,8},{10,9},{11,10},{12... | collective-permute-start | bytes 589832 | tf_op jit(solution)/shard_map/while/body/eval_jaxpr/ppermute | solution.py:10
  7.9 7.0 %collective-permute-start.1 = (bf16[768,128]{1,0:T(8,128)(2,1)S(1)}, bf16[768,128]{1,0:T(8,128)(2,1)S(1)}, u32[]{:S(2)}, u32[]{:S(2)}) collective-permute-start(bf16[768,128]{1,0:T(8,128)(2,1)S(1)} %copy.19), channel_id=1, source_target_pairs={{1,0},{2,1},{3,2},{4,3},{5,4},{6,5},{7,6},{9,8},{10,9},{11,10},{12... | collective-permute-start | bytes 589832 | tf_op jit(solution)/shard_map/while/body/eval_jaxpr/ppermute | solution.py:10
  18.8 5.1 %collective-permute-start.1 = (bf16[768,128]{1,0:T(8,128)(2,1)S(1)}, bf16[768,128]{1,0:T(8,128)(2,1)S(1)}, u32[]{:S(2)}, u32[]{:S(2)}) collective-permute-start(bf16[768,128]{1,0:T(8,128)(2,1)S(1)} %copy.19), channel_id=1, source_target_pairs={{1,0},{2,1},{3,2},{4,3},{5,4},{6,5},{7,6},{9,8},{10,9},{11,10},{12... | collective-permute-start | bytes 589832 | tf_op jit(solution)/shard_map/while/body/eval_jaxpr/ppermute | solution.py:10
  27.7 7.0 %collective-permute-start.1 = (bf16[768,128]{1,0:T(8,128)(2,1)S(1)}, bf16[768,128]{1,0:T(8,128)(2,1)S(1)}, u32[]{:S(2)}, u32[]{:S(2)}) collective-permute-start(bf16[768,128]{1,0:T(8,128)(2,1)S(1)} %copy.19), channel_id=1, source_target_pairs={{1,0},{2,1},{3,2},{4,3},{5,4},{6,5},{7,6},{9,8},{10,9},{11,10},{12... | collective-permute-start | bytes 589832 | tf_op jit(solution)/shard_map/while/body/eval_jaxpr/ppermute | solution.py:10
  38.6 7.0 %collective-permute-start.1 = (bf16[768,128]{1,0:T(8,128)(2,1)S(1)}, bf16[768,128]{1,0:T(8,128)(2,1)S(1)}, u32[]{:S(2)}, u32[]{:S(2)}) collective-permute-start(bf16[768,128]{1,0:T(8,128)(2,1)S(1)} %copy.19), channel_id=1, source_target_pairs={{1,0},{2,1},{3,2},{4,3},{5,4},{6,5},{7,6},{9,8},{10,9},{11,10},{12... | collective-permute-start | bytes 589832 | tf_op jit(solution)/shard_map/while/body/eval_jaxpr/ppermute | solution.py:10
  49.5 7.0 %collective-permute-start.1 = (bf16[768,128]{1,0:T(8,128)(2,1)S(1)}, bf16[768,128]{1,0:T(8,128)(2,1)S(1)}, u32[]{:S(2)}, u32[]{:S(2)}) collective-permute-start(bf16[768,128]{1,0:T(8,128)(2,1)S(1)} %copy.19), channel_id=1, source_target_pairs={{1,0},{2,1},{3,2},{4,3},{5,4},{6,5},{7,6},{9,8},{10,9},{11,10},{12... | collective-permute-start | bytes 589832 | tf_op jit(solution)/shard_map/while/body/eval_jaxpr/ppermute | solution.py:10
  56.6 10.7 %collective-permute-start.1 = (bf16[768,128]{1,0:T(8,128)(2,1)S(1)}, bf16[768,128]{1,0:T(8,128)(2,1)S(1)}, u32[]{:S(2)}, u32[]{:S(2)}) collective-permute-start(bf16[768,128]{1,0:T(8,128)(2,1)S(1)} %copy.19), channel_id=1, source_target_pairs={{1,0},{2,1},{3,2},{4,3},{5,4},{6,5},{7,6},{9,8},{10,9},{11,10},{12... | collective-permute-start | bytes 589832 | tf_op jit(solution)/shard_map/while/body/eval_jaxpr/ppermute | solution.py:10
  67.5 7.0 %collective-permute-start.1 = (bf16[768,128]{1,0:T(8,128)(2,1)S(1)}, bf16[768,128]{1,0:T(8,128)(2,1)S(1)}, u32[]{:S(2)}, u32[]{:S(2)}) collective-permute-start(bf16[768,128]{1,0:T(8,128)(2,1)S(1)} %copy.19), channel_id=1, source_target_pairs={{1,0},{2,1},{3,2},{4,3},{5,4},{6,5},{7,6},{9,8},{10,9},{11,10},{12... | collective-permute-start | bytes 589832 | tf_op jit(solution)/shard_map/while/body/eval_jaxpr/ppermute | solution.py:10
  74.7 7.0 %collective-permute-start.1 = (bf16[768,128]{1,0:T(8,128)(2,1)S(1)}, bf16[768,128]{1,0:T(8,128)(2,1)S(1)}, u32[]{:S(2)}, u32[]{:S(2)}) collective-permute-start(bf16[768,128]{1,0:T(8,128)(2,1)S(1)} %copy.19), channel_id=1, source_target_pairs={{1,0},{2,1},{3,2},{4,3},{5,4},{6,5},{7,6},{9,8},{10,9},{11,10},{12... | collective-permute-start | bytes 589832 | tf_op jit(solution)/shard_map/while/body/eval_jaxpr/ppermute | solution.py:10
  81.8 7.0 %collective-permute-start.1 = (bf16[768,128]{1,0:T(8,128)(2,1)S(1)}, bf16[768,128]{1,0:T(8,128)(2,1)S(1)}, u32[]{:S(2)}, u32[]{:S(2)}) collective-permute-start(bf16[768,128]{1,0:T(8,128)(2,1)S(1)} %copy.19), channel_id=1, source_target_pairs={{1,0},{2,1},{3,2},{4,3},{5,4},{6,5},{7,6},{9,8},{10,9},{11,10},{12... | collective-permute-start | bytes 589832 | tf_op jit(solution)/shard_map/while/body/eval_jaxpr/ppermute | solution.py:10
  89.0 7.0 %collective-permute-start.1 = (bf16[768,128]{1,0:T(8,128)(2,1)S(1)}, bf16[768,128]{1,0:T(8,128)(2,1)S(1)}, u32[]{:S(2)}, u32[]{:S(2)}) collective-permute-start(bf16[768,128]{1,0:T(8,128)(2,1)S(1)} %copy.19), channel_id=1, source_target_pairs={{1,0},{2,1},{3,2},{4,3},{5,4},{6,5},{7,6},{9,8},{10,9},{11,10},{12... | collective-permute-start | bytes 589832 | tf_op jit(solution)/shard_map/while/body/eval_jaxpr/ppermute | solution.py:10
  96.2 7.2 %collective-permute-start = (bf16[768,128]{1,0:T(8,128)(2,1)S(1)}, bf16[768,128]{1,0:T(8,128)(2,1)S(1)}, u32[]{:S(2)}, u32[]{:S(2)}) collective-permute-start(bf16[768,128]{1,0:T(8,128)(2,1)S(1)} %copy.18), channel_id=1, source_target_pairs={{0,1},{1,2},{2,3},{3,4},{4,5},{5,6},{6,7},{8,9},{9,10},{10,11},{11... | collective-permute-start | bytes 589832 | tf_op jit(solution)/shard_map/while/body/eval_jaxpr/ppermute | solution.py:10
  103.5 7.0 %collective-permute-start = (bf16[768,128]{1,0:T(8,128)(2,1)S(1)}, bf16[768,128]{1,0:T(8,128)(2,1)S(1)}, u32[]{:S(2)}, u32[]{:S(2)}) collective-permute-start(bf16[768,128]{1,0:T(8,128)(2,1)S(1)} %copy.18), channel_id=1, source_target_pairs={{0,1},{1,2},{2,3},{3,4},{4,5},{5,6},{6,7},{8,9},{9,10},{10,11},{11... | collective-permute-start | bytes 589832 | tf_op jit(solution)/shard_map/while/body/eval_jaxpr/ppermute | solution.py:10
  110.7 7.0 %collective-permute-start = (bf16[768,128]{1,0:T(8,128)(2,1)S(1)}, bf16[768,128]{1,0:T(8,128)(2,1)S(1)}, u32[]{:S(2)}, u32[]{:S(2)}) collective-permute-start(bf16[768,128]{1,0:T(8,128)(2,1)S(1)} %copy.18), channel_id=1, source_target_pairs={{0,1},{1,2},{2,3},{3,4},{4,5},{5,6},{6,7},{8,9},{9,10},{10,11},{11... | collective-permute-start | bytes 589832 | tf_op jit(solution)/shard_map/while/body/eval_jaxpr/ppermute | solution.py:10
  117.8 7.0 %collective-permute-start = (bf16[768,128]{1,0:T(8,128)(2,1)S(1)}, bf16[768,128]{1,0:T(8,128)(2,1)S(1)}, u32[]{:S(2)}, u32[]{:S(2)}) collective-permute-start(bf16[768,128]{1,0:T(8,128)(2,1)S(1)} %copy.18), channel_id=1, source_target_pairs={{0,1},{1,2},{2,3},{3,4},{4,5},{5,6},{6,7},{8,9},{9,10},{10,11},{11... | collective-permute-start | bytes 589832 | tf_op jit(solution)/shard_map/while/body/eval_jaxpr/ppermute | solution.py:10
  125.0 7.0 %collective-permute-start = (bf16[768,128]{1,0:T(8,128)(2,1)S(1)}, bf16[768,128]{1,0:T(8,128)(2,1)S(1)}, u32[]{:S(2)}, u32[]{:S(2)}) collective-permute-start(bf16[768,128]{1,0:T(8,128)(2,1)S(1)} %copy.18), channel_id=1, source_target_pairs={{0,1},{1,2},{2,3},{3,4},{4,5},{5,6},{6,7},{8,9},{9,10},{10,11},{11... | collective-permute-start | bytes 589832 | tf_op jit(solution)/shard_map/while/body/eval_jaxpr/ppermute | solution.py:10
  132.1 7.0 %collective-permute-start = (bf16[768,128]{1,0:T(8,128)(2,1)S(1)}, bf16[768,128]{1,0:T(8,128)(2,1)S(1)}, u32[]{:S(2)}, u32[]{:S(2)}) collective-permute-start(bf16[768,128]{1,0:T(8,128)(2,1)S(1)} %copy.18), channel_id=1, source_target_pairs={{0,1},{1,2},{2,3},{3,4},{4,5},{5,6},{6,7},{8,9},{9,10},{10,11},{11... | collective-permute-start | bytes 589832 | tf_op jit(solution)/shard_map/while/body/eval_jaxpr/ppermute | solution.py:10
  139.3 20.0 %collective-permute-start = (bf16[768,128]{1,0:T(8,128)(2,1)S(1)}, bf16[768,128]{1,0:T(8,128)(2,1)S(1)}, u32[]{:S(2)}, u32[]{:S(2)}) collective-permute-start(bf16[768,128]{1,0:T(8,128)(2,1)S(1)} %copy.18), channel_id=1, source_target_pairs={{0,1},{1,2},{2,3},{3,4},{4,5},{5,6},{6,7},{8,9},{9,10},{10,11},{11... | collective-permute-start | bytes 589832 | tf_op jit(solution)/shard_map/while/body/eval_jaxpr/ppermute | solution.py:10
  163.3 7.0 %collective-permute-start = (bf16[768,128]{1,0:T(8,128)(2,1)S(1)}, bf16[768,128]{1,0:T(8,128)(2,1)S(1)}, u32[]{:S(2)}, u32[]{:S(2)}) collective-permute-start(bf16[768,128]{1,0:T(8,128)(2,1)S(1)} %copy.18), channel_id=1, source_target_pairs={{0,1},{1,2},{2,3},{3,4},{4,5},{5,6},{6,7},{8,9},{9,10},{10,11},{11... | collective-permute-start | bytes 589832 | tf_op jit(solution)/shard_map/while/body/eval_jaxpr/ppermute | solution.py:10
  174.4 7.0 %collective-permute-start = (bf16[768,128]{1,0:T(8,128)(2,1)S(1)}, bf16[768,128]{1,0:T(8,128)(2,1)S(1)}, u32[]{:S(2)}, u32[]{:S(2)}) collective-permute-start(bf16[768,128]{1,0:T(8,128)(2,1)S(1)} %copy.18), channel_id=1, source_target_pairs={{0,1},{1,2},{2,3},{3,4},{4,5},{5,6},{6,7},{8,9},{9,10},{10,11},{11... | collective-permute-start | bytes 589832 | tf_op jit(solution)/shard_map/while/body/eval_jaxpr/ppermute | solution.py:10
  185.5 7.0 %collective-permute-start = (bf16[768,128]{1,0:T(8,128)(2,1)S(1)}, bf16[768,128]{1,0:T(8,128)(2,1)S(1)}, u32[]{:S(2)}, u32[]{:S(2)}) collective-permute-start(bf16[768,128]{1,0:T(8,128)(2,1)S(1)} %copy.18), channel_id=1, source_target_pairs={{0,1},{1,2},{2,3},{3,4},{4,5},{5,6},{6,7},{8,9},{9,10},{10,11},{11... | collective-permute-start | bytes 589832 | tf_op jit(solution)/shard_map/while/body/eval_jaxpr/ppermute | solution.py:10
  196.6 7.0 %collective-permute-start = (bf16[768,128]{1,0:T(8,128)(2,1)S(1)}, bf16[768,128]{1,0:T(8,128)(2,1)S(1)}, u32[]{:S(2)}, u32[]{:S(2)}) collective-permute-start(bf16[768,128]{1,0:T(8,128)(2,1)S(1)} %copy.18), channel_id=1, source_target_pairs={{0,1},{1,2},{2,3},{3,4},{4,5},{5,6},{6,7},{8,9},{9,10},{10,11},{11... | collective-permute-start | bytes 589832 | tf_op jit(solution)/shard_map/while/body/eval_jaxpr/ppermute | solution.py:10
